TPU v7x, 32 devices: a whole 2x2x4 slice. The times are simulated.
32 devices in a mesh: clips: 2 (over y), tm: 4 (over z), rows: 4 (over x, core).
Axes of the slice: x: 2, y: 2, z: 4, core: 2. Of those that a mesh axis runs over, the one named last changes fastest.
Arguments:
- latents: bfloat16 [32, 8, 192, 128], P(('clips', 'tm'), 'rows'), parts along dimension 0, may hold values from -6 to 6
- conv_weight: bfloat16 [3, 27, 192, 192], replicated, may hold values from -0.078125 to 0.078125
- norm_gains: float32 [3, 192], replicated, may hold values from 0.5 to 1.5
- biases: float32 [3, 192], replicated, may hold values from -3 to 3
Outputs:
- decoded: bfloat16 [32, 8, 192, 128], P(('clips', 'tm'), 'rows'), parts along dimension 0
There are 2 independent parts, one for each index of `clips`. A program takes and returns all parts, laid end to end along the dimension named above; an argument that names none is the same for every part. Nothing has to cross between parts.
All inputs are finite; a program needn't handle non-finite values.
Results may differ from a plain program's by a relative error of at most 0.011.
Values may be sent and summed in bfloat16 or wider, within the bound.
A program may use at most 64 MiB of HBM per device.

v0:
```python
import jax
import jax.numpy as jnp
from jax import lax
from jax.sharding import PartitionSpec as P

LAYERS = 3


EPSILON = 1e-06


def passed_along(block, axis, distance):
    devices = range(lax.axis_size(axis))
    route = [(i - distance, i) for i in devices if i - distance in devices]
    return lax.ppermute(block, axis, route)


def padded_2(cells, sides, width):
    for axis, dim in sides:
        count = lax.axis_size(axis)
        ends = count - 1
        head = lax.slice_in_dim(cells, 0, width, axis=dim)
        tail = lax.slice_in_dim(cells, cells.shape[dim] - width, cells.shape[dim], axis=dim)
        cells = jnp.concatenate(
            [
                lax.ppermute(tail, axis, [(i, (i + 1) % count) for i in range(ends)]),
                cells,
                lax.ppermute(head, axis, [((i + 1) % count, i) for i in range(ends)]),
            ],
            axis=dim,
        )
    return cells


def activate(values, gain_row):
    widened = values.astype(jnp.float32)
    squares = jnp.mean(widened * widened, axis=2, keepdims=True)
    normed = widened * lax.rsqrt(squares + EPSILON) * gain_row[None, None, :, None]
    return jax.nn.silu(normed).astype(jnp.bfloat16)


def surround(values):
    trailing = passed_along(values[-2:], "tm", 1)
    joined = jnp.concatenate([trailing, values], axis=0)
    return padded_2(joined, (("rows", 1),), 1)


def convolve(padded, weight, frames, row_count):
    total = None
    for column_tap in range(3):
        partial_sum = None
        for time_tap in range(3):
            for row_tap in range(3):
                window = padded[time_tap : time_tap + frames, row_tap : row_tap + row_count]
                product = jnp.einsum(
                    "oc,fhcw->fhow",
                    weight[9 * time_tap + 3 * row_tap + column_tap],
                    window,
                    preferred_element_type=jnp.float32,
                )
                partial_sum = product if partial_sum is None else partial_sum + product
        zero_column = jnp.zeros(partial_sum.shape[:3] + (1,), jnp.float32)
        if column_tap == 0:
            partial_sum = jnp.concatenate([zero_column, partial_sum[..., :-1]], axis=3)
        elif column_tap == 2:
            partial_sum = jnp.concatenate([partial_sum[..., 1:], zero_column], axis=3)
        total = partial_sum if total is None else total + partial_sum
    return total


def on_device(latents, conv_weight, norm_gains, biases):
    values = latents
    frames = values.shape[0]
    row_count = values.shape[1]
    for layer_index in range(LAYERS):
        padded = surround(activate(values, norm_gains[layer_index]))
        total = convolve(padded, conv_weight[layer_index], frames, row_count)
        summed = values.astype(jnp.float32) + total + biases[layer_index][None, None, :, None]
        values = summed.astype(jnp.bfloat16)
    return values


def solution(mesh):
    in_specs = (P(("clips", "tm"), "rows", None, None), P(), P(), P())
    out_specs = P(("clips", "tm"), "rows", None, None)
    return jax.shard_map(
        on_device, mesh=mesh, in_specs=in_specs, out_specs=out_specs, check_vma=False
    )
```

profile of v0, /device:TPU:9, one launch (start us, length us, event | category | flops | bytes accessed | tf_op | source)
XLA Modules:
  0.0 79.3 jit_solution(3278248625686851769)
XLA Ops:
  0.0 0.9 %fusion.386 = (f32[1,192]{1,0:T(1,128)S(1)}, f32[1,192]{1,0:T(1,128)S(1)}, f32[1,192]{1,0:T(1,128)S(1)}) fusion(f32[3,192]{1,0:T(4,128)} %param.6), kind=kLoop, calls=%fused_computation.431 | loop fusion | bytes 4608 | tf_op jit(solution)/shard_map/slice | solution.py:76
  0.9 1.2 %fusion.80 = f32[4,2,128]{2,1,0:T(2,128)S(1)} fusion(bf16[4,2,192,128]{3,2,1,0:T(8,128)(2,1)} %param.4), kind=kLoop, calls=%fused_computation.115 | loop fusion | flops 588800 | bytes 397312 | tf_op jit(solution)/shard_map/reduce_sum | solution.py:37
  2.1 1.6 %fusion.87 = bf16[4,2,192,128]{3,2,1,0:T(8,128)(2,1)S(1)} fusion(bf16[4,2,192,128]{3,2,1,0:T(8,128)(2,1)} %param.4, f32[192]{0:T(256)S(1)} %bitcast.645, f32[4,2,128]{2,1,0:T(2,128)S(1)} %add_rsqrt_fusion.2), kind=kLoop, calls=%fused_computation.122 | loop fusion | flops 1572864 | bytes 791296 | tf_op jit(solution)/shard_map/convert_element_type | solution.py:39
  3.8 3.2 %collective-permute-start = (bf16[2,2,192,128]{3,2,1,0:T(8,128)(2,1)S(1)}, bf16[2,2,192,128]{3,2,1,0:T(8,128)(2,1)S(1)}, u32[]{:S(2)}, u32[]{:S(2)}) collective-permute-start(bf16[2,2,192,128]{3,2,1,0:T(8,128)(2,1)S(1)} %slice.735), channel_id=1, source_target_pairs={{0,4},{4,8},{8,12},{1,5},{5,9},{9,13},{2,6},{6,10},{10,14},{3,7},{... | collective-permute-start | bytes 589832 | tf_op jit(solution)/shard_map/ppermute | solution.py:15
  7.0 1.2 %fusion.284 = f32[4,2,128,192]{2,3,1,0:T(8,128)S(1)} fusion(bf16[4,2,192,128]{3,2,1,0:T(8,128)(2,1)S(1)} %fusion.87, bf16[3,27,192,192]{3,2,1,0:T(8,128)(2,1)} %param.5), kind=kOutput, calls=%fused_computation.335 | convolution fusion | flops 75497472 | bytes 1277952 | tf_op jit(solution)/shard_map/oc,fhcw->fhow/dot_general | solution.py:55
  8.1 1.2 %fusion.272 = f32[4,2,128,192]{2,3,1,0:T(8,128)S(1)} fusion(bf16[4,2,192,128]{3,2,1,0:T(8,128)(2,1)S(1)} %fusion.87, bf16[3,27,192,192]{3,2,1,0:T(8,128)(2,1)} %param.5), kind=kOutput, calls=%fused_computation.323 | convolution fusion | flops 75497472 | bytes 1277952 | tf_op jit(solution)/shard_map/oc,fhcw->fhow/dot_general | solution.py:55
  9.3 1.2 %fusion.260 = f32[4,2,128,192]{2,3,1,0:T(8,128)S(1)} fusion(bf16[4,2,192,128]{3,2,1,0:T(8,128)(2,1)S(1)} %fusion.87, bf16[3,27,192,192]{3,2,1,0:T(8,128)(2,1)} %param.5), kind=kOutput, calls=%fused_computation.311 | convolution fusion | flops 75497472 | bytes 1277952 | tf_op jit(solution)/shard_map/oc,fhcw->fhow/dot_general | solution.py:55
  10.5 0.8 %fusion.385 = (f32[1,192]{1,0:T(1,128)S(1)}, f32[1,192]{1,0:T(1,128)S(1)}, f32[1,192]{1,0:T(1,128)S(1)}) fusion(f32[3,192]{1,0:T(4,128)} %param.7), kind=kLoop, calls=%fused_computation.430 | loop fusion | bytes 4608 | tf_op jit(solution)/shard_map/slice | solution.py:78
  11.5 4.5 %collective-permute-start.1 = (bf16[6,1,192,128]{3,2,1,0:T(8,128)(2,1)S(1)}, bf16[6,1,192,128]{3,2,1,0:T(8,128)(2,1)S(1)}, u32[]{:S(2)}, u32[]{:S(2)}) collective-permute-start(bf16[6,1,192,128]{3,2,1,0:T(8,128)(2,1)S(1)} %get-tuple-element.16), channel_id=1, source_target_pairs={{0,1},{1,2},{2,3},{4,5},{5,6},{6,7},{8,9},{9,10},{10,11},{12,13},{... | collective-permute-start | bytes 884744 | tf_op jit(solution)/shard_map/ppermute | solution.py:26
  16.0 1.9 %collective-permute-start.2 = (bf16[6,1,192,128]{3,2,1,0:T(8,128)(2,1)S(1)}, bf16[6,1,192,128]{3,2,1,0:T(8,128)(2,1)S(1)}, u32[]{:S(2)}, u32[]{:S(2)}) collective-permute-start(bf16[6,1,192,128]{3,2,1,0:T(8,128)(2,1)S(1)} %get-tuple-element.15), channel_id=1, source_target_pairs={{1,0},{2,1},{3,2},{5,4},{6,5},{7,6},{9,8},{10,9},{11,10},{13,12},{... | collective-permute-start | bytes 884744 | tf_op jit(solution)/shard_map/ppermute | solution.py:28
  18.0 1.2 %fusion.288 = f32[4,2,128,192]{2,3,1,0:T(8,128)S(1)} fusion(bf16[3,27,192,192]{3,2,1,0:T(8,128)(2,1)} %param.5, bf16[4,2,192,128]{3,2,1,0:T(8,128)(2,1)S(1)} %fusion.87, bf16[2,2,192,128]{3,2,1,0:T(8,128)(2,1)S(1)} %collective-permute-done), kind=kOutput, calls=%fused_computation.339 | convolution fusion | flops 76283904 | bytes 1474560 | tf_op jit(solution)/shard_map/oc,fhcw->fhow/dot_general | solution.py:55
  20.5 3.6 %collective-permute-done.2 = bf16[6,1,192,128]{3,2,1,0:T(8,128)(2,1)S(1)} collective-permute-done((bf16[6,1,192,128]{3,2,1,0:T(8,128)(2,1)S(1)}, bf16[6,1,192,128]{3,2,1,0:T(8,128)(2,1)S(1)}, u32[]{:S(2)}, u32[]{:S(2)}) %collective-permute-start.2) | collective-permute-done | bytes 294944 | tf_op jit(solution)/shard_map/ppermute | solution.py:28
  31.0 3.2 %collective-permute-start.3 = (bf16[2,2,192,128]{3,2,1,0:T(8,128)(2,1)S(1)}, bf16[2,2,192,128]{3,2,1,0:T(8,128)(2,1)S(1)}, u32[]{:S(2)}, u32[]{:S(2)}) collective-permute-start(bf16[2,2,192,128]{3,2,1,0:T(8,128)(2,1)S(1)} %slice.750), channel_id=1, source_target_pairs={{0,4},{4,8},{8,12},{1,5},{5,9},{9,13},{2,6},{6,10},{10,14},{3,7},{... | collective-permute-start | bytes 589832 | tf_op jit(solution)/shard_map/ppermute | solution.py:15
  34.4 2.9 %collective-permute-done.3 = bf16[2,2,192,128]{3,2,1,0:T(8,128)(2,1)S(1)} collective-permute-done((bf16[2,2,192,128]{3,2,1,0:T(8,128)(2,1)S(1)}, bf16[2,2,192,128]{3,2,1,0:T(8,128)(2,1)S(1)}, u32[]{:S(2)}, u32[]{:S(2)}) %collective-permute-start.3) | collective-permute-done | bytes 196640 | tf_op jit(solution)/shard_map/ppermute | solution.py:15
  37.4 2.9 %collective-permute-start.4 = (bf16[6,1,192,128]{3,2,1,0:T(8,128)(2,1)S(1)}, bf16[6,1,192,128]{3,2,1,0:T(8,128)(2,1)S(1)}, u32[]{:S(2)}, u32[]{:S(2)}) collective-permute-start(bf16[6,1,192,128]{3,2,1,0:T(8,128)(2,1)S(1)} %get-tuple-element.12), channel_id=1, source_target_pairs={{0,1},{1,2},{2,3},{4,5},{5,6},{6,7},{8,9},{9,10},{10,11},{12,13},{... | collective-permute-start | bytes 884744 | tf_op jit(solution)/shard_map/ppermute | solution.py:26
  40.3 2.1 %collective-permute-start.5 = (bf16[6,1,192,128]{3,2,1,0:T(8,128)(2,1)S(1)}, bf16[6,1,192,128]{3,2,1,0:T(8,128)(2,1)S(1)}, u32[]{:S(2)}, u32[]{:S(2)}) collective-permute-start(bf16[6,1,192,128]{3,2,1,0:T(8,128)(2,1)S(1)} %get-tuple-element.11), channel_id=1, source_target_pairs={{1,0},{2,1},{3,2},{5,4},{6,5},{7,6},{9,8},{10,9},{11,10},{13,12},{... | collective-permute-start | bytes 884744 | tf_op jit(solution)/shard_map/ppermute | solution.py:28
  44.0 4.4 %collective-permute-done.5 = bf16[6,1,192,128]{3,2,1,0:T(8,128)(2,1)S(1)} collective-permute-done((bf16[6,1,192,128]{3,2,1,0:T(8,128)(2,1)S(1)}, bf16[6,1,192,128]{3,2,1,0:T(8,128)(2,1)S(1)}, u32[]{:S(2)}, u32[]{:S(2)}) %collective-permute-start.5) | collective-permute-done | bytes 294944 | tf_op jit(solution)/shard_map/ppermute | solution.py:28
  53.3 0.6 fusion.42
  55.2 3.2 %collective-permute-start.6 = (bf16[2,2,192,128]{3,2,1,0:T(8,128)(2,1)S(1)}, bf16[2,2,192,128]{3,2,1,0:T(8,128)(2,1)S(1)}, u32[]{:S(2)}, u32[]{:S(2)}) collective-permute-start(bf16[2,2,192,128]{3,2,1,0:T(8,128)(2,1)S(1)} %slice.765), channel_id=1, source_target_pairs={{0,4},{4,8},{8,12},{1,5},{5,9},{9,13},{2,6},{6,10},{10,14},{3,7},{... | collective-permute-start | bytes 589832 | tf_op jit(solution)/shard_map/ppermute | solution.py:15
  58.7 2.9 %collective-permute-done.6 = bf16[2,2,192,128]{3,2,1,0:T(8,128)(2,1)S(1)} collective-permute-done((bf16[2,2,192,128]{3,2,1,0:T(8,128)(2,1)S(1)}, bf16[2,2,192,128]{3,2,1,0:T(8,128)(2,1)S(1)}, u32[]{:S(2)}, u32[]{:S(2)}) %collective-permute-start.6) | collective-permute-done | bytes 196640 | tf_op jit(solution)/shard_map/ppermute | solution.py:15
  61.7 2.9 %collective-permute-start.7 = (bf16[6,1,192,128]{3,2,1,0:T(8,128)(2,1)S(1)}, bf16[6,1,192,128]{3,2,1,0:T(8,128)(2,1)S(1)}, u32[]{:S(2)}, u32[]{:S(2)}) collective-permute-start(bf16[6,1,192,128]{3,2,1,0:T(8,128)(2,1)S(1)} %get-tuple-element.8), channel_id=1, source_target_pairs={{0,1},{1,2},{2,3},{4,5},{5,6},{6,7},{8,9},{9,10},{10,11},{12,13},{... | collective-permute-start | bytes 884744 | tf_op jit(solution)/shard_map/ppermute | solution.py:26
  64.6 1.9 %collective-permute-start.8 = (bf16[6,1,192,128]{3,2,1,0:T(8,128)(2,1)S(1)}, bf16[6,1,192,128]{3,2,1,0:T(8,128)(2,1)S(1)}, u32[]{:S(2)}, u32[]{:S(2)}) collective-permute-start(bf16[6,1,192,128]{3,2,1,0:T(8,128)(2,1)S(1)} %get-tuple-element.7), channel_id=1, source_target_pairs={{1,0},{2,1},{3,2},{5,4},{6,5},{7,6},{9,8},{10,9},{11,10},{13,12},{... | collective-permute-start | bytes 884744 | tf_op jit(solution)/shard_map/ppermute | solution.py:28
  68.3 4.4 %collective-permute-done.8 = bf16[6,1,192,128]{3,2,1,0:T(8,128)(2,1)S(1)} collective-permute-done((bf16[6,1,192,128]{3,2,1,0:T(8,128)(2,1)S(1)}, bf16[6,1,192,128]{3,2,1,0:T(8,128)(2,1)S(1)}, u32[]{:S(2)}, u32[]{:S(2)}) %collective-permute-start.8) | collective-permute-done | bytes 294944 | tf_op jit(solution)/shard_map/ppermute | solution.py:28
  78.2 1.2 %fusion.79 = bf16[4,2,192,128]{3,2,1,0:T(8,128)(2,1)} fusion(f32[4,2,192,128]{3,2,1,0:T(8,128)S(1)} %get-tuple-element.26, f32[4,2,128,192]{2,3,1,0:T(8,128)S(1)} %fusion.17, f32[4,2,192,127]{3,2,1,0:T(8,128)S(1)} %slice.779, f32[4,2,192,127]{3,2,1,0:T(8,128)S(1)} %bitcast.641, f32[192]{0:T(256)S(1)} %bitcast.644, ...), kind=kOutput, calls=%fused_computation.97 | convolution fusion | flops 76677120 | bytes 4031488 | tf_op jit(solution)/shard_map/oc,fhcw->fhow/dot_general | solution.py:55
  (100 shorter events, 23.7 us)
Async XLA Ops:
  0.0 19.1 %copy-start = (bf16[3,27,192,192]{3,2,1,0:T(8,128)(2,1)S(1)}, bf16[3,27,192,192]{3,2,1,0:T(8,128)(2,1)}, u32[]{:S(2)}) copy-start(bf16[3,27,192,192]{3,2,1,0:T(8,128)(2,1)} %param.5) | copy-start | bytes 17915908
  3.8 7.7 %collective-permute-start = (bf16[2,2,192,128]{3,2,1,0:T(8,128)(2,1)S(1)}, bf16[2,2,192,128]{3,2,1,0:T(8,128)(2,1)S(1)}, u32[]{:S(2)}, u32[]{:S(2)}) collective-permute-start(bf16[2,2,192,128]{3,2,1,0:T(8,128)(2,1)S(1)} %slice.735), channel_id=1, source_target_pairs={{0,4},{4,8},{8,12},{1,5},{5,9},{9,13},{2,6},{6,10},{10,14},{3,7},{... | collective-permute-start | bytes 589832 | tf_op jit(solution)/shard_map/ppermute | solution.py:15
  11.5 8.9 %collective-permute-start.1 = (bf16[6,1,192,128]{3,2,1,0:T(8,128)(2,1)S(1)}, bf16[6,1,192,128]{3,2,1,0:T(8,128)(2,1)S(1)}, u32[]{:S(2)}, u32[]{:S(2)}) collective-permute-start(bf16[6,1,192,128]{3,2,1,0:T(8,128)(2,1)S(1)} %get-tuple-element.16), channel_id=1, source_target_pairs={{0,1},{1,2},{2,3},{4,5},{5,6},{6,7},{8,9},{9,10},{10,11},{12,13},{... | collective-permute-start | bytes 884744 | tf_op jit(solution)/shard_map/ppermute | solution.py:26
  16.0 8.0 %collective-permute-start.2 = (bf16[6,1,192,128]{3,2,1,0:T(8,128)(2,1)S(1)}, bf16[6,1,192,128]{3,2,1,0:T(8,128)(2,1)S(1)}, u32[]{:S(2)}, u32[]{:S(2)}) collective-permute-start(bf16[6,1,192,128]{3,2,1,0:T(8,128)(2,1)S(1)} %get-tuple-element.15), channel_id=1, source_target_pairs={{1,0},{2,1},{3,2},{5,4},{6,5},{7,6},{9,8},{10,9},{11,10},{13,12},{... | collective-permute-start | bytes 884744 | tf_op jit(solution)/shard_map/ppermute | solution.py:28
  28.1 1.6 %copy-start.1 = (bf16[4,2,192,128]{3,2,1,0:T(8,128)(2,1)S(1)}, bf16[4,2,192,128]{3,2,1,0:T(8,128)(2,1)}, u32[]{:S(2)}) copy-start(bf16[4,2,192,128]{3,2,1,0:T(8,128)(2,1)} %param.4) | copy-start | bytes 1179652
  31.0 6.4 %collective-permute-start.3 = (bf16[2,2,192,128]{3,2,1,0:T(8,128)(2,1)S(1)}, bf16[2,2,192,128]{3,2,1,0:T(8,128)(2,1)S(1)}, u32[]{:S(2)}, u32[]{:S(2)}) collective-permute-start(bf16[2,2,192,128]{3,2,1,0:T(8,128)(2,1)S(1)} %slice.750), channel_id=1, source_target_pairs={{0,4},{4,8},{8,12},{1,5},{5,9},{9,13},{2,6},{6,10},{10,14},{3,7},{... | collective-permute-start | bytes 589832 | tf_op jit(solution)/shard_map/ppermute | solution.py:15
  37.4 6.6 %collective-permute-start.4 = (bf16[6,1,192,128]{3,2,1,0:T(8,128)(2,1)S(1)}, bf16[6,1,192,128]{3,2,1,0:T(8,128)(2,1)S(1)}, u32[]{:S(2)}, u32[]{:S(2)}) collective-permute-start(bf16[6,1,192,128]{3,2,1,0:T(8,128)(2,1)S(1)} %get-tuple-element.12), channel_id=1, source_target_pairs={{0,1},{1,2},{2,3},{4,5},{5,6},{6,7},{8,9},{9,10},{10,11},{12,13},{... | collective-permute-start | bytes 884744 | tf_op jit(solution)/shard_map/ppermute | solution.py:26
  40.3 8.0 %collective-permute-start.5 = (bf16[6,1,192,128]{3,2,1,0:T(8,128)(2,1)S(1)}, bf16[6,1,192,128]{3,2,1,0:T(8,128)(2,1)S(1)}, u32[]{:S(2)}, u32[]{:S(2)}) collective-permute-start(bf16[6,1,192,128]{3,2,1,0:T(8,128)(2,1)S(1)} %get-tuple-element.11), channel_id=1, source_target_pairs={{1,0},{2,1},{3,2},{5,4},{6,5},{7,6},{9,8},{10,9},{11,10},{13,12},{... | collective-permute-start | bytes 884744 | tf_op jit(solution)/shard_map/ppermute | solution.py:28
  55.2 6.4 %collective-permute-start.6 = (bf16[2,2,192,128]{3,2,1,0:T(8,128)(2,1)S(1)}, bf16[2,2,192,128]{3,2,1,0:T(8,128)(2,1)S(1)}, u32[]{:S(2)}, u32[]{:S(2)}) collective-permute-start(bf16[2,2,192,128]{3,2,1,0:T(8,128)(2,1)S(1)} %slice.765), channel_id=1, source_target_pairs={{0,4},{4,8},{8,12},{1,5},{5,9},{9,13},{2,6},{6,10},{10,14},{3,7},{... | collective-permute-start | bytes 589832 | tf_op jit(solution)/shard_map/ppermute | solution.py:15
  61.7 6.6 %collective-permute-start.7 = (bf16[6,1,192,128]{3,2,1,0:T(8,128)(2,1)S(1)}, bf16[6,1,192,128]{3,2,1,0:T(8,128)(2,1)S(1)}, u32[]{:S(2)}, u32[]{:S(2)}) collective-permute-start(bf16[6,1,192,128]{3,2,1,0:T(8,128)(2,1)S(1)} %get-tuple-element.8), channel_id=1, source_target_pairs={{0,1},{1,2},{2,3},{4,5},{5,6},{6,7},{8,9},{9,10},{10,11},{12,13},{... | collective-permute-start | bytes 884744 | tf_op jit(solution)/shard_map/ppermute | solution.py:26
  64.6 8.0 %collective-permute-start.8 = (bf16[6,1,192,128]{3,2,1,0:T(8,128)(2,1)S(1)}, bf16[6,1,192,128]{3,2,1,0:T(8,128)(2,1)S(1)}, u32[]{:S(2)}, u32[]{:S(2)}) collective-permute-start(bf16[6,1,192,128]{3,2,1,0:T(8,128)(2,1)S(1)} %get-tuple-element.7), channel_id=1, source_target_pairs={{1,0},{2,1},{3,2},{5,4},{6,5},{7,6},{9,8},{10,9},{11,10},{13,12},{... | collective-permute-start | bytes 884744 | tf_op jit(solution)/shard_map/ppermute | solution.py:28
where the time goes:
time: 79.8 us; the launch traced here: 79.3 us
  matrix products  27.7 us (35%)
  starting transfers between devices  25.9 us (32%)
  waiting for transfers between devices  18.6 us (23%)
  other arithmetic  3.99 us (5%)
  local copies, waits for them, and re-layouts  2.54 us (3%)
    dot_general x81, matrix products, convolve(): jnp.einsum('oc,fhcw->fhow', weight[9 * time_tap + 3 * row_tap + column_ta...  27.7 us
    ppermute x3, waiting for transfers between devices, padded_2(): lax.ppermute(head, axis, [((i + 1) % count, i) for i in range(ends)])  12.4 us
    ppermute x3, starting transfers between devices, padded_2(): lax.ppermute(tail, axis, [(i, (i + 1) % count) for i in range(ends)])  10.3 us
    ppermute x3, starting transfers between devices, passed_along(): return lax.ppermute(block, axis, route)  9.6 us
    ppermute x3, waiting for transfers between devices, passed_along(): return lax.ppermute(block, axis, route)  6.08 us
    ppermute x3, starting transfers between devices, padded_2(): lax.ppermute(head, axis, [((i + 1) % count, i) for i in range(ends)])  5.94 us
    convert_element_type x3, other arithmetic, activate(): return jax.nn.silu(normed).astype(jnp.bfloat16)  2.23 us
  transfers between devices with their start and end apart: 9, of which 7 were waited for; matrix products, arithmetic and copies ran while one was open for 13% of the time, Pallas kernels for 0%

commit v1 on v0

v1 whole, which is shorter than its diff:
```python
import functools

import jax
import jax.numpy as jnp
from jax import lax
from jax.experimental import pallas as pl
from jax.experimental.pallas import tpu as pltpu
from jax.sharding import PartitionSpec as P

EPSILON = 1e-06
MESH = pl.DeviceIdType.MESH

TM, UP = 0, 2


def stack_kernel(
    layers, frames, rows_here, channels, columns,
    x_ref, w_hbm, gains_ref, biases_ref, out_ref,
    w_raw, w_cat, act, values, gain_col, bias_col,
    w_sem, send_sem, recv_sem,
):
    tm, tm_count = lax.axis_index("tm"), lax.axis_size("tm")
    row, row_count = lax.axis_index("rows"), lax.axis_size("rows")
    has_prev, has_next = tm > 0, tm < tm_count - 1
    has_up, has_down = row > 0, row < row_count - 1
    last_row = rows_here
    DOWN = UP + frames + 2

    def weights(layer):
        return pltpu.make_async_copy(w_hbm.at[layer], w_raw.at[layer], w_sem.at[layer])

    for layer in range(layers):
        weights(layer).start()

    barrier = pltpu.get_barrier_semaphore()
    for there, target in (
        (has_prev, {"tm": tm - 1}),
        (has_next, {"tm": tm + 1}),
        (has_up, {"rows": row - 1}),
        (has_down, {"rows": row + 1}),
    ):
        @pl.when(there)
        def _(target=target):
            pl.semaphore_signal(barrier, inc=1, device_id=target, device_id_type=MESH)

    def tm_copy(layer, frame):
        at = frame - (frames - 2)
        return pltpu.make_async_remote_copy(
            src_ref=act.at[layer, frame + 2, pl.ds(1, rows_here)],
            dst_ref=act.at[layer, at, pl.ds(1, rows_here)],
            send_sem=send_sem.at[layer, TM + at],
            recv_sem=recv_sem.at[layer, TM + at],
            device_id={"tm": tm + 1},
            device_id_type=MESH,
        )

    def up_copy(layer, padded):
        return pltpu.make_async_remote_copy(
            src_ref=act.at[layer, padded, 1],
            dst_ref=act.at[layer, padded, last_row + 1],
            send_sem=send_sem.at[layer, UP + padded],
            recv_sem=recv_sem.at[layer, UP + padded],
            device_id={"rows": row - 1},
            device_id_type=MESH,
        )

    def down_copy(layer, padded):
        return pltpu.make_async_remote_copy(
            src_ref=act.at[layer, padded, last_row],
            dst_ref=act.at[layer, padded, 0],
            send_sem=send_sem.at[layer, DOWN + padded],
            recv_sem=recv_sem.at[layer, DOWN + padded],
            device_id={"rows": row + 1},
            device_id_type=MESH,
        )

    def send_rows(layer, padded):
        @pl.when(has_up)
        def _():
            up_copy(layer, padded).start()

        @pl.when(has_down)
        def _():
            down_copy(layer, padded).start()

    def wait_rows(layer, padded):
        @pl.when(has_down)
        def _():
            up_copy(layer, padded).wait_recv()

        @pl.when(has_up)
        def _():
            down_copy(layer, padded).wait_recv()

    def activate(layer, frame, value):
        squares = jnp.mean(value * value, axis=1, keepdims=True)
        normed = value * lax.rsqrt(squares + EPSILON) * gain_col[layer][None]
        act[layer, frame + 2, pl.ds(1, rows_here)] = (
            normed / (1.0 + jnp.exp(-normed))
        ).astype(jnp.bfloat16)

    def send_frame(layer, frame):
        if frame >= frames - 2:
            @pl.when(has_next)
            def _():
                tm_copy(layer, frame).start()
        send_rows(layer, frame + 2)

    def relay(layer, at):
        @pl.when(has_prev)
        def _():
            tm_copy(layer, at + frames - 2).wait_recv()
            send_rows(layer, at)

    def prepare(layer):
        weights(layer).wait()
        taps = w_raw.shape[1] // 3
        for c in range(3):
            for first in range(0, taps, 2):
                count = min(2, taps - first)
                tiles = [w_raw[layer, 3 * (first + n) + c] for n in range(count)]
                block = jnp.concatenate(tiles, axis=1) if count > 1 else tiles[0]
                w_cat[
                    layer,
                    c * channels:(c + 1) * channels,
                    first * channels:(first + count) * channels,
                ] = block

    def columns_of(ref, layer):
        line = ref[pl.ds(layer, 1), :]
        return jnp.transpose(jnp.broadcast_to(line, (columns, channels)))

    for layer in range(layers):
        gain_col[layer] = columns_of(gains_ref, layer)
        bias_col[layer] = columns_of(biases_ref, layer)

    for frame in range(frames - 1, -1, -1):
        activate(0, frame, x_ref[frame].astype(jnp.float32))

    greeted = sum(there.astype(jnp.int32) for there in (has_prev, has_next, has_up, has_down))
    pl.semaphore_wait(barrier, greeted)
    for frame in range(frames - 1, -1, -1):
        send_frame(0, frame)

    zero_frame = jnp.zeros((channels, columns), jnp.bfloat16)
    for layer in range(layers):
        @pl.when(jnp.logical_not(has_prev))
        def _(layer=layer):
            for at in range(2):
                for h in range(rows_here + 2):
                    act[layer, at, h] = zero_frame

        @pl.when(jnp.logical_and(has_prev, jnp.logical_not(has_up)))
        def _(layer=layer):
            for at in range(2):
                act[layer, at, 0] = zero_frame

        @pl.when(jnp.logical_and(has_prev, jnp.logical_not(has_down)))
        def _(layer=layer):
            for at in range(2):
                act[layer, at, last_row + 1] = zero_frame

        @pl.when(jnp.logical_not(has_up))
        def _(layer=layer):
            for at in range(frames):
                act[layer, at + 2, 0] = zero_frame

        @pl.when(jnp.logical_not(has_down))
        def _(layer=layer):
            for at in range(frames):
                act[layer, at + 2, last_row + 1] = zero_frame

    prepare(0)

    lane = lax.broadcasted_iota(jnp.int32, (channels, columns), 1)
    not_first, not_last = lane > 0, lane < columns - 1
    depth = 9 * channels

    def convolve(layer, frame):
        rhs = jnp.concatenate(
            [
                act[layer, frame:frame + 3, h:h + 3].reshape(depth, columns)
                for h in range(rows_here)
            ],
            axis=1,
        )
        product = jnp.dot(w_cat[layer], rhs, preferred_element_type=jnp.float32)
        results = []
        for h in range(rows_here):
            part = product[:, h * columns:(h + 1) * columns]
            left = pltpu.roll(part[:channels], 1, 1)
            right = pltpu.roll(part[2 * channels:], columns - 1, 1)
            total = part[channels:2 * channels]
            total = total + jnp.where(not_first, left, 0.0)
            total = total + jnp.where(not_last, right, 0.0)
            before = x_ref[frame, h] if layer == 0 else values[frame, h]
            summed = before.astype(jnp.float32) + total + bias_col[layer]
            results.append(summed.astype(jnp.bfloat16))
        return results

    for layer in range(layers):
        for frame in range(frames - 1, -1, -1):
            if frame == 2:
                relay(layer, 1)
            if frame == 1:
                relay(layer, 0)
                if layer == 0:
                    for later in range(1, layers):
                        prepare(later)
            if frame == frames - 1:
                for padded in range(frames + 1, frame - 1, -1):
                    wait_rows(layer, padded)
            elif frame >= 2:
                wait_rows(layer, frame)
            else:
                @pl.when(has_prev)
                def _(layer=layer, frame=frame):
                    wait_rows(layer, frame)
            results = convolve(layer, frame)
            if layer == layers - 1:
                for h in range(rows_here):
                    out_ref[frame, h] = results[h]
            else:
                for h in range(rows_here):
                    values[frame, h] = results[h]
                activate(layer + 1, frame, jnp.stack(results).astype(jnp.float32))
                send_frame(layer + 1, frame)

    for layer in range(layers):
        for frame in (frames - 1, frames - 2):
            @pl.when(has_next)
            def _(layer=layer, frame=frame):
                tm_copy(layer, frame).wait_send()
        for padded in range(frames + 2):
            there = True if padded >= 2 else has_prev

            @pl.when(jnp.logical_and(has_up, there))
            def _(layer=layer, padded=padded):
                up_copy(layer, padded).wait_send()

            @pl.when(jnp.logical_and(has_down, there))
            def _(layer=layer, padded=padded):
                down_copy(layer, padded).wait_send()


def on_device(latents, conv_weight, norm_gains, biases):
    frames, rows_here, channels, columns = latents.shape
    layers, taps = conv_weight.shape[:2]
    kinds = 2 + 2 * (frames + 2)
    vmem = pl.BlockSpec(memory_space=pltpu.VMEM)
    return pl.pallas_call(
        functools.partial(stack_kernel, layers, frames, rows_here, channels, columns),
        out_shape=jax.ShapeDtypeStruct(latents.shape, latents.dtype),
        in_specs=[vmem, pl.BlockSpec(memory_space=pl.ANY), vmem, vmem],
        out_specs=vmem,
        scratch_shapes=[
            pltpu.VMEM((layers, taps, channels, channels), jnp.bfloat16),
            pltpu.VMEM((layers, 3 * channels, 9 * channels), jnp.bfloat16),
            pltpu.VMEM((layers, frames + 2, rows_here + 2, channels, columns), jnp.bfloat16),
            pltpu.VMEM((frames, rows_here, channels, columns), jnp.bfloat16),
            pltpu.VMEM((layers, channels, columns), jnp.float32),
            pltpu.VMEM((layers, channels, columns), jnp.float32),
            pltpu.SemaphoreType.DMA((layers,)),
            pltpu.SemaphoreType.DMA((layers, kinds)),
            pltpu.SemaphoreType.DMA((layers, kinds)),
        ],
        compiler_params=pltpu.CompilerParams(collective_id=0, has_side_effects=True),
        name="conv_stack",
    )(latents, conv_weight, norm_gains, biases)


def solution(mesh):
    in_specs = (P(("clips", "tm"), "rows", None, None), P(), P(), P())
    out_specs = P(("clips", "tm"), "rows", None, None)
    return jax.shard_map(
        on_device, mesh=mesh, in_specs=in_specs, out_specs=out_specs, check_vma=False
    )
```

time: 79.8 us -> 34.1 us (0.43)
  Pallas kernels: 0 us -> 32.1 us
  matrix products: 27.7 us -> 0 us
  starting transfers between devices: 25.9 us -> 0 us
  waiting for transfers between devices: 18.6 us -> 0 us
  other arithmetic: 3.99 us -> 0 us
    pallas_call x0 -> x1, Pallas kernels: none -> 32.1 us  [on_device(): pl.pallas_call(functools.partial(stack_kernel, layers, frames, rows_here,...]
    dot_general x81 -> x0, matrix products: 27.7 us -> none  [convolve(): jnp.einsum('oc,fhcw->fhow', weight[9 * time_tap + 3 * row_tap + column_ta...]
    ppermute x9 -> x0, starting transfers between devices: 25.9 us -> none  [the longest x3 10.3 us: padded_2(): lax.ppermute(tail, axis, [(i, (i + 1) % count) for i in range(ends)])]
    ppermute x9 -> x0, waiting for transfers between devices: 18.6 us -> none  [the longest x3 12.4 us: padded_2(): lax.ppermute(head, axis, [((i + 1) % count, i) for i in range(ends)])]
    slice x8 -> x0, local copies, waits for them, and re-layouts: 2.53 us -> none  [the longest x1 0.87 us: on_device(): padded = surround(activate(values, norm_gains[layer_index]))]
    convert_element_type x3 -> x0, other arithmetic: 2.23 us -> none  [activate(): return jax.nn.silu(normed).astype(jnp.bfloat16)]
    unnamed x4 -> x1, local copies, waits for them, and re-layouts: 0.01 us -> 1.77 us
    reduce_sum x1 -> x0, other arithmetic: 1.21 us -> none  [activate(): squares = jnp.mean(widened * widened, axis=2, keepdims=True)]
  transfers between devices with their start and end apart: 9 -> 0, of which waited for: 7 -> 0; matrix products, arithmetic and copies ran while one was open for 13% -> 0% of each run, Pallas kernels for 0% -> 0%
where the time goes in v1:
time: 34.1 us; the launch traced here: 33.9 us
  Pallas kernels  32.1 us (94%)
  local copies, waits for them, and re-layouts  1.77 us (5%)
    pallas_call x1, Pallas kernels, on_device(): pl.pallas_call(functools.partial(stack_kernel, layers, frames, rows_here,...  32.1 us
    unnamed x1, local copies, waits for them, and re-layouts  1.77 us

profile of v1, /device:TPU:9, one launch (start us, length us, event | category | flops | bytes accessed | tf_op | source)
XLA Modules:
  0.0 33.9 jit_solution(9170350313959789937)
XLA Ops:
  0.0 32.1 %conv_stack.1 = bf16[4,2,192,128]{3,2,1,0:T(8,128)(2,1)} custom-call(bf16[4,2,192,128]{3,2,1,0:T(8,128)(2,1)} %x_ref.1, bf16[3,27,192,192]{3,2,1,0:T(8,128)(2,1)} %w_hbm.1, f32[3,192]{1,0:T(4,128)} %gains_ref.1, f32[3,192]{1,0:T(4,128)} %biases_ref.1), custom_call_target="tpu_custom_call" | custom-call | tf_op jit(solution)/shard_map/conv_stack/pallas_call | solution.py:251
  32.1 1.8 %copy.6 = bf16[4,2,192,128]{3,2,1,0:T(8,128)(2,1)} copy(bf16[4,2,192,128]{3,2,1,0:T(8,128)(2,1)} %conv_stack.1) | data formatting | bytes 786432

commit v2 on v1

--- a/solution.py
+++ b/solution.py
@@ -16,7 +16,7 @@
 def stack_kernel(
     layers, frames, rows_here, channels, columns,
     x_ref, w_hbm, gains_ref, biases_ref, out_ref,
-    w_raw, w_cat, act, values, gain_col, bias_col,
+    w_raw, w_cat, early, products, act, values, gain_col, bias_col,
     w_sem, send_sem, recv_sem,
 ):
     tm, tm_count = lax.axis_index("tm"), lax.axis_size("tm")
@@ -94,9 +94,9 @@
 
     def activate(layer, frame, value):
         squares = jnp.mean(value * value, axis=1, keepdims=True)
-        normed = value * lax.rsqrt(squares + EPSILON) * gain_col[layer][None]
+        half = value * lax.rsqrt(squares + EPSILON) * gain_col[layer][None]
         act[layer, frame + 2, pl.ds(1, rows_here)] = (
-            normed / (1.0 + jnp.exp(-normed))
+            half + half * jnp.tanh(half)
         ).astype(jnp.bfloat16)
 
     def send_frame(layer, frame):
@@ -115,10 +115,11 @@
     def prepare(layer):
         weights(layer).wait()
         taps = w_raw.shape[1] // 3
+        order = [3 * a + b for a in (2, 1, 0) for b in range(3)]
         for c in range(3):
             for first in range(0, taps, 2):
                 count = min(2, taps - first)
-                tiles = [w_raw[layer, 3 * (first + n) + c] for n in range(count)]
+                tiles = [w_raw[layer, 3 * order[first + n] + c] for n in range(count)]
                 block = jnp.concatenate(tiles, axis=1) if count > 1 else tiles[0]
                 w_cat[
                     layer,
@@ -130,17 +131,18 @@
         line = ref[pl.ds(layer, 1), :]
         return jnp.transpose(jnp.broadcast_to(line, (columns, channels)))
 
-    for layer in range(layers):
-        gain_col[layer] = columns_of(gains_ref, layer)
-        bias_col[layer] = columns_of(biases_ref, layer)
-
-    for frame in range(frames - 1, -1, -1):
-        activate(0, frame, x_ref[frame].astype(jnp.float32))
-
+    gain_col[0] = 0.5 * columns_of(gains_ref, 0)
+    activate(0, frames - 1, x_ref[frames - 1].astype(jnp.float32))
     greeted = sum(there.astype(jnp.int32) for there in (has_prev, has_next, has_up, has_down))
     pl.semaphore_wait(barrier, greeted)
-    for frame in range(frames - 1, -1, -1):
+    send_frame(0, frames - 1)
+    for frame in range(frames - 2, -1, -1):
+        activate(0, frame, x_ref[frame].astype(jnp.float32))
         send_frame(0, frame)
+    for layer in range(layers):
+        if layer > 0:
+            gain_col[layer] = 0.5 * columns_of(gains_ref, layer)
+        bias_col[layer] = columns_of(biases_ref, layer)
 
     zero_frame = jnp.zeros((channels, columns), jnp.bfloat16)
     for layer in range(layers):
@@ -174,17 +176,42 @@
 
     lane = lax.broadcasted_iota(jnp.int32, (channels, columns), 1)
     not_first, not_last = lane > 0, lane < columns - 1
-    depth = 9 * channels
-
-    def convolve(layer, frame):
-        rhs = jnp.concatenate(
+    local_depth = 6 * channels
+
+    def windows(layer, frame, taps):
+        return jnp.concatenate(
             [
-                act[layer, frame:frame + 3, h:h + 3].reshape(depth, columns)
+                jnp.concatenate(
+                    [
+                        act[layer, frame + a, h:h + 3].reshape(3 * channels, columns)
+                        for a in taps
+                    ],
+                    axis=0,
+                )
                 for h in range(rows_here)
             ],
             axis=1,
         )
-        product = jnp.dot(w_cat[layer], rhs, preferred_element_type=jnp.float32)
+
+    def local_part(layer, frame):
+        early[...] = jnp.dot(
+            w_cat[layer, :, :local_depth],
+            windows(layer, frame, (2, 1)),
+            preferred_element_type=jnp.float32,
+        )
+
+    def multiply(layer, frame, resumed):
+        if resumed:
+            return early[...] + jnp.dot(
+                w_cat[layer, :, local_depth:],
+                windows(layer, frame, (0,)),
+                preferred_element_type=jnp.float32,
+            )
+        return jnp.dot(
+            w_cat[layer], windows(layer, frame, (2, 1, 0)), preferred_element_type=jnp.float32
+        )
+
+    def finish(layer, frame, product):
         results = []
         for h in range(rows_here):
             part = product[:, h * columns:(h + 1) * columns]
@@ -196,17 +223,33 @@
             before = x_ref[frame, h] if layer == 0 else values[frame, h]
             summed = before.astype(jnp.float32) + total + bias_col[layer]
             results.append(summed.astype(jnp.bfloat16))
-        return results
-
-    for layer in range(layers):
+        into = out_ref if layer == layers - 1 else values
+        for h in range(rows_here):
+            into[frame, h] = results[h]
+        if layer < layers - 1:
+            activate(layer + 1, frame, jnp.stack(results).astype(jnp.float32))
+
+    def send_next(layer, frame):
+        if layer < layers - 1:
+            send_frame(layer + 1, frame)
+
+    for layer in range(layers):
+        pending = None
         for frame in range(frames - 1, -1, -1):
-            if frame == 2:
+            resumed = layer == 0 and frame == 1
+            late = frame <= 1
+            if frame == (1 if layer == 0 else 2):
                 relay(layer, 1)
+            if resumed:
+                for later in range(1, layers):
+                    prepare(later)
+                local_part(layer, frame)
+                if pending is not None:
+                    finish(layer, pending, products[pending % 2])
+                    send_next(layer, pending)
+                    pending = None
             if frame == 1:
                 relay(layer, 0)
-                if layer == 0:
-                    for later in range(1, layers):
-                        prepare(later)
             if frame == frames - 1:
                 for padded in range(frames + 1, frame - 1, -1):
                     wait_rows(layer, padded)
@@ -216,15 +259,21 @@
                 @pl.when(has_prev)
                 def _(layer=layer, frame=frame):
                     wait_rows(layer, frame)
-            results = convolve(layer, frame)
-            if layer == layers - 1:
-                for h in range(rows_here):
-                    out_ref[frame, h] = results[h]
+            product = multiply(layer, frame, resumed)
+            if pending is not None:
+                finish(layer, pending, products[pending % 2])
+            hold = frame > 0 if layer == layers - 1 else not late
+            if hold:
+                products[frame % 2] = product
             else:
-                for h in range(rows_here):
-                    values[frame, h] = results[h]
-                activate(layer + 1, frame, jnp.stack(results).astype(jnp.float32))
-                send_frame(layer + 1, frame)
+                finish(layer, frame, product)
+            if pending is not None:
+                send_next(layer, pending)
+                pending = None
+            if hold:
+                pending = frame
+            else:
+                send_next(layer, frame)
 
     for layer in range(layers):
         for frame in (frames - 1, frames - 2):
@@ -256,6 +305,8 @@
         scratch_shapes=[
             pltpu.VMEM((layers, taps, channels, channels), jnp.bfloat16),
             pltpu.VMEM((layers, 3 * channels, 9 * channels), jnp.bfloat16),
+            pltpu.VMEM((3 * channels, rows_here * columns), jnp.float32),
+            pltpu.VMEM((2, 3 * channels, rows_here * columns), jnp.float32),
             pltpu.VMEM((layers, frames + 2, rows_here + 2, channels, columns), jnp.bfloat16),
             pltpu.VMEM((frames, rows_here, channels, columns), jnp.bfloat16),
             pltpu.VMEM((layers, channels, columns), jnp.float32),

time: 34.1 us -> 34.5 us (1.012)
  no operation moved by 1% of the time
where the time goes in v2:
time: 34.5 us; the launch traced here: 34 us
  Pallas kernels  32.2 us (93%)
  local copies, waits for them, and re-layouts  1.77 us (5%)
    pallas_call x1, Pallas kernels, on_device(): pl.pallas_call(functools.partial(stack_kernel, layers, frames, rows_here,...  32.2 us
    unnamed x1, local copies, waits for them, and re-layouts  1.77 us

profile of v2, /device:TPU:9, one launch (start us, length us, event | category | flops | bytes accessed | tf_op | source)
XLA Modules:
  0.0 34.0 jit_solution(10334628415380250575)
XLA Ops:
  0.0 32.2 %conv_stack.1 = bf16[4,2,192,128]{3,2,1,0:T(8,128)(2,1)} custom-call(bf16[4,2,192,128]{3,2,1,0:T(8,128)(2,1)} %x_ref.1, bf16[3,27,192,192]{3,2,1,0:T(8,128)(2,1)} %w_hbm.1, f32[3,192]{1,0:T(4,128)} %gains_ref.1, f32[3,192]{1,0:T(4,128)} %biases_ref.1), custom_call_target="tpu_custom_call" | custom-call | tf_op jit(solution)/shard_map/conv_stack/pallas_call | solution.py:300
  32.2 1.8 %copy.6 = bf16[4,2,192,128]{3,2,1,0:T(8,128)(2,1)} copy(bf16[4,2,192,128]{3,2,1,0:T(8,128)(2,1)} %conv_stack.1) | data formatting | bytes 786432

commit v3 on v2

--- a/solution.py
+++ b/solution.py
@@ -237,8 +237,7 @@
         pending = None
         for frame in range(frames - 1, -1, -1):
             resumed = layer == 0 and frame == 1
-            late = frame <= 1
-            if frame == (1 if layer == 0 else 2):
+            if layer == 0 and frame == 1:
                 relay(layer, 1)
             if resumed:
                 for later in range(1, layers):
@@ -248,7 +247,7 @@
                     finish(layer, pending, products[pending % 2])
                     send_next(layer, pending)
                     pending = None
-            if frame == 1:
+            if layer == 0 and frame == 1:
                 relay(layer, 0)
             if frame == frames - 1:
                 for padded in range(frames + 1, frame - 1, -1):
@@ -259,10 +258,12 @@
                 @pl.when(has_prev)
                 def _(layer=layer, frame=frame):
                     wait_rows(layer, frame)
+            if layer > 0 and frame >= frames - 2:
+                relay(layer, frame - (frames - 2))
             product = multiply(layer, frame, resumed)
             if pending is not None:
                 finish(layer, pending, products[pending % 2])
-            hold = frame > 0 if layer == layers - 1 else not late
+            hold = layer == layers - 1 and frame > 0
             if hold:
                 products[frame % 2] = product
             else:

time: 34.5 us -> 32.7 us (0.948); the launches traced: 34 us -> 32.5 us
  Pallas kernels: 32.2 us -> 30.7 us
    pallas_call x1, Pallas kernels: 32.2 us -> 30.7 us  [on_device(): pl.pallas_call(functools.partial(stack_kernel, layers, frames, rows_here,...]
where the time goes in v3:
time: 32.7 us; the launch traced here: 32.5 us
  Pallas kernels  30.7 us (94%)
  local copies, waits for them, and re-layouts  1.77 us (5%)
    pallas_call x1, Pallas kernels, on_device(): pl.pallas_call(functools.partial(stack_kernel, layers, frames, rows_here,...  30.7 us
    unnamed x1, local copies, waits for them, and re-layouts  1.77 us

profile of v3, /device:TPU:9, one launch (start us, length us, event | category | flops | bytes accessed | tf_op | source)
XLA Modules:
  0.0 32.5 jit_solution(1975489269234947354)
XLA Ops:
  0.0 30.7 %conv_stack.1 = bf16[4,2,192,128]{3,2,1,0:T(8,128)(2,1)} custom-call(bf16[4,2,192,128]{3,2,1,0:T(8,128)(2,1)} %x_ref.1, bf16[3,27,192,192]{3,2,1,0:T(8,128)(2,1)} %w_hbm.1, f32[3,192]{1,0:T(4,128)} %gains_ref.1, f32[3,192]{1,0:T(4,128)} %biases_ref.1), custom_call_target="tpu_custom_call" | custom-call | tf_op jit(solution)/shard_map/conv_stack/pallas_call | solution.py:301
  30.8 1.8 %copy.6 = bf16[4,2,192,128]{3,2,1,0:T(8,128)(2,1)} copy(bf16[4,2,192,128]{3,2,1,0:T(8,128)(2,1)} %conv_stack.1) | data formatting | bytes 786432
